TPU v7x, 256 devices: a whole 4x4x8 slice. The times are simulated.
256 devices in a mesh: seq: 64 (over y, z, core), tab: 4 (over x).
Axes of the slice: x: 4, y: 4, z: 8, core: 2. Of those that a mesh axis runs over, the one named last changes fastest.
Arguments:
- cotangent: bfloat16 [65536, 2560], P('seq', 'tab'), may hold values from -6 to 6
- saved_value: bfloat16 [65536, 2560], P('seq', 'tab'), may hold values from -6 to 6
- gate_scale: float32 [65536], P('seq'), may hold values from 0.2 to 1
- conv_weight: float32 [4, 2560], P(None, 'tab'), may hold values from -3 to 3
- value_weight: bfloat16 [1280, 2560], P(None, 'tab'), may hold values from -0.25 to 0.25
- owner_ids: int32 [8, 65536, 1], P('tab', 'seq'), may hold values from 0 to 63; in each aligned block of 1024 rows (0 to 1023, 1024 to 2047, ..., all dimensions but the last counted through in order) at most 64 rows name the same one
- local_row: int32 [8, 65536], P('tab', 'seq'), may hold values from 0 to 511
- row_table: float32 [8, 32768, 160], P('tab', 'seq'), may hold values from -6 to 6
- moment_one: float32 [8, 32768, 160], P('tab', 'seq'), may hold values from -6 to 6
- moment_two: float32 [8, 32768, 160], P('tab', 'seq'), may hold values from 0.5 to 4
Outputs:
- new_table: float32 [8, 32768, 160], P('tab', 'seq')
- new_first: float32 [8, 32768, 160], P('tab', 'seq')
- new_second: float32 [8, 32768, 160], P('tab', 'seq')
Inputs may be any that keep to these rules, and one draw needn't show every extreme that they name: `owner_ids`: within each aligned block of 1024 tokens of one head (one device's tokens), no owner is named by more than 64 tokens; in some blocks one owner is named by exactly 64.
All inputs are finite; a program needn't handle non-finite values.
Results may differ from a plain program's by a relative error of at most 0.0029.
Values may be sent and summed in bfloat16 or wider, within the bound.
No kernel may reach another device: no remote copies, remote signals or barrier semaphores. Data moves between devices by JAX's collectives and lax.ppermute only.
A program may use at most 128 MiB of HBM per device.

v0:
```python
import jax
import jax.numpy as jnp
from jax import lax
from jax.sharding import PartitionSpec as P

beta_one = 0.9
beta_two = 0.95
learn_rate = 0.01
adam_steps = 10.0
epsilon = 1e-08


def from_behind(block, axis, distance):
    devices = range(lax.axis_size(axis))
    route = [(i - distance, i) for i in devices if i - distance in devices]
    return lax.ppermute(block, axis, route)


def causal_mix(context, conv_weight, length):
    mix_total = jnp.zeros((length, context.shape[1]), jnp.float32)
    for tap_index in range(4):
        row_start = 9 - 3 * tap_index
        mix_total = (
            mix_total + conv_weight[tap_index][None, :] * context[row_start : row_start + length]
        )
    return mix_total


def conv_adjoint(upstream, mixed_conv):
    squashed = jax.nn.sigmoid(mixed_conv)
    return upstream * squashed * (1.0 + mixed_conv * (1.0 - squashed))


def shards(
    cotangent,
    saved_value,
    gate_scale,
    conv_weight,
    value_weight,
    owner_ids,
    local_row,
    row_table,
    moment_one,
    moment_two,
):
    length = cotangent.shape[0]
    head_local = row_table.shape[0]
    table_rows = row_table.shape[1]
    head_dim = row_table.shape[2]
    own_width = head_local * head_dim
    peer_count = lax.axis_size("seq")
    count_cap = 4 * length // peer_count
    upstream = cotangent.astype(jnp.float32)
    value_rows = saved_value.astype(jnp.float32)
    prior_rows = from_behind(saved_value[length - 9 :], "seq", 1)
    context = jnp.concatenate([prior_rows.astype(jnp.float32), value_rows], axis=0)
    conv_grad = conv_adjoint(upstream, causal_mix(context, conv_weight, length))
    following = from_behind(conv_grad[:9], "seq", -1)
    extended = jnp.concatenate([conv_grad, following], axis=0)
    value_grad = upstream
    for tap_index in range(4):
        row_start = 3 * tap_index
        value_grad = (
            value_grad + conv_weight[tap_index][None, :] * extended[row_start : row_start + length]
        )
    scaled = (gate_scale[:, None] * value_grad).astype(jnp.bfloat16)
    full_term = lax.dot_general(
        value_weight, scaled, (((1,), (1,)), ((), ())), preferred_element_type=jnp.float32
    )
    summed = lax.psum(full_term, "tab")
    memory_grad = lax.dynamic_slice_in_dim(summed, lax.axis_index("tab") * own_width, own_width, 0)
    heads_grad = jnp.swapaxes(memory_grad.reshape(head_local, head_dim, length), 1, 2)
    owners = owner_ids[:, :, 0]
    position = jnp.arange(length, dtype=jnp.int32)
    earlier = position[None, :] < position[:, None]
    same_owner = owners[:, :, None] == owners[:, None, :]
    slot_rank = jnp.sum((same_owner & earlier[None]).astype(jnp.int32), axis=2)
    slot_index = owners * count_cap + slot_rank
    head_ids = jnp.broadcast_to(jnp.arange(head_local, dtype=jnp.int32)[:, None], slot_index.shape)
    send_grad = (
        jnp.zeros((head_local, peer_count * count_cap, head_dim), jnp.float32)
        .at[head_ids, slot_index]
        .set(heads_grad)
    )
    send_rows = (
        jnp.zeros((head_local, peer_count * count_cap), jnp.int32)
        .at[head_ids, slot_index]
        .set(local_row + 1)
    )
    send_grad = send_grad.reshape(head_local, peer_count, count_cap, head_dim)
    send_rows = send_rows.reshape(head_local, peer_count, count_cap)
    grads_in = lax.all_to_all(send_grad, "seq", split_axis=1, concat_axis=1, tiled=True)
    rows_in = lax.all_to_all(send_rows, "seq", split_axis=1, concat_axis=1, tiled=True)
    item_count = grads_in.shape[0]
    flat_rows = rows_in.reshape(item_count, -1) - 1
    flat_grads = grads_in.reshape(item_count, -1, head_dim)
    item_ids = jnp.broadcast_to(jnp.arange(item_count, dtype=jnp.int32)[:, None], flat_rows.shape)
    target = jnp.where(flat_rows < 0, table_rows, flat_rows)
    summed_rows = (
        jnp.zeros((item_count, table_rows, head_dim), jnp.float32)
        .at[item_ids, target]
        .add(flat_grads, mode="drop")
    )
    row_hits = (
        jnp.zeros((item_count, table_rows), jnp.int32).at[item_ids, target].add(1, mode="drop")
    )
    row_grad, row_hits = (summed_rows, row_hits)
    touched = (row_hits > 0)[:, :, None]
    first_next = beta_one * moment_one + (1.0 - beta_one) * row_grad
    second_next = beta_two * moment_two + (1.0 - beta_two) * row_grad * row_grad
    update = (
        first_next
        / (1.0 - beta_one**adam_steps)
        / (jnp.sqrt(second_next / (1.0 - beta_two**adam_steps)) + epsilon)
    )
    table_next = row_table - learn_rate * update
    return (
        jnp.where(touched, table_next, row_table),
        jnp.where(touched, first_next, moment_one),
        jnp.where(touched, second_next, moment_two),
    )


def solution(mesh):
    in_specs = (
        P("seq", "tab"),
        P("seq", "tab"),
        P("seq"),
        P(None, "tab"),
        P(None, "tab"),
        P("tab", "seq", None),
        P("tab", "seq"),
        P("tab", "seq", None),
        P("tab", "seq", None),
        P("tab", "seq", None),
    )
    out_specs = (P("tab", "seq", None), P("tab", "seq", None), P("tab", "seq", None))
    return jax.shard_map(shards, mesh=mesh, in_specs=in_specs, out_specs=out_specs, check_vma=False)
```

profile of v0, /device:TPU:1, one launch (start us, length us, event | category | flops | bytes accessed | tf_op | source)
XLA Modules:
  0.0 436.1 jit_solution(14999547283841224572)
XLA Ops:
  7.2 0.9 slice.42
  8.1 4.9 %collective-permute-start = (bf16[9,640]{1,0:T(8,128)(2,1)S(1)}, bf16[9,640]{1,0:T(8,128)(2,1)S(1)}, u32[]{:S(2)}, u32[]{:S(2)}) collective-permute-start(bf16[9,640]{1,0:T(8,128)(2,1)S(1)} %slice.42), channel_id=1, source_target_pairs={{0,4},{4,8},{8,12},{12,16},{16,20},{20,24},{24,28},{28,32},{32,36}... | collective-permute-start | bytes 34568 | tf_op jit(solution)/shard_map/ppermute | solution.py:16
  13.0 0.9 slice_reduce_fusion.3
  13.9 1.5 convert_element_type.17
  15.5 2.1 fusion.2
  17.6 1.9 collective-permute-start.1
  19.5 3.4 collective-permute-done.1
  22.9 6.8 %convolution_bitcast_fusion = f32[1280,1024]{0,1:T(8,128)} fusion(bf16[1280,640]{1,0:T(8,128)(2,1)S(1)} %copy-done, bf16[1024,640]{1,0:T(8,128)(2,1)S(1)} %copy-done.2, f32[9,640]{1,0:T(8,128)S(1)} %collective-permute-done.1, f32[1024,640]{1,0:T(8,128)S(1)} %fusion.2, f32[640]{0:T(1024)S(1)} %get-tuple-element.23, f32[640]{0:T(1024)S(1)} %get-tuple-element.24, ...), kind=kOutput, calls=%fused_computation.5 | convolution fusion | flops 1686896640 | bytes 10850816 | tf_op jit(solution)/shard_map/dot_general | solution.py:67
  29.7 0.7 copy-done.4
  30.4 0.3 iota_compare_fusion
  30.7 1.9 convert_reduce_fusion
  32.9 8.1 %scatter_custom_fusion = s32[8192]{0:T(1024)S(1)} fusion(s32[2048]{0:T(1024)S(1)} %get-tuple-element.29, s32[2048]{0:T(1024)S(1)} %get-tuple-element.28, s32[]{:T(128)} %constant.19.clone.1), kind=kCustom, calls=%fused_computation.60 | custom fusion | bytes 32772
  41.1 0.7 reshape.147
  41.8 11.6 %all-to-all-start = ((s32[64,1,128]{2,1,0:T(1,128)}), s32[64,1,128]{2,1,0:T(1,128)S(1)}, u32[]{:S(2)}, u32[]{:S(2)}) async-start(s32[64,1,128]{2,1,0:T(1,128)} %reshape.147), calls=%async_computation | async-start | bytes 65536 | tf_op jit(solution)/shard_map/all_to_all | solution.py:93
  53.5 93.5 %all-reduce.2.cloned.1.call-done = f32[1280,1024]{0,1:T(8,128)} async-done(((f32[1280,1024]{0,1:T(8,128)}), f32[1280,1024]{0,1:T(8,128)}) %all-reduce.2.cloned.1.call-update) | async-done | bytes 5242896 | tf_op jit(solution)/shard_map/psum | solution.py:70
  146.9 2.1 constant_dynamic-slice_fusion
  149.0 0.5 copy.100
  149.5 1.8 copy.116
  151.3 13.2 %scatter_custom_fusion.2 = f32[8192,160]{1,0:T(8,128)} fusion(s32[2048]{0:T(1024)S(1)} %get-tuple-element.29, f32[2048,160]{1,0:T(8,128)} %bitcast.36, f32[]{:T(128)} %constant.26.clone.1), kind=kCustom, calls=%fused_computation.6 | custom fusion | bytes 5243392
  164.5 7.7 %copy.104 = f32[2,64,64,160]{3,2,0,1:T(8,128)} copy(f32[2,64,64,160]{3,2,1,0:T(8,128)} %bitcast.32) | data formatting | bytes 10485760 | tf_op jit(solution)/shard_map/reshape | solution.py:90
  172.2 11.2 %all-to-all-start.1 = ((f32[2,64,64,160]{3,2,0,1:T(8,128)}), f32[2,64,64,160]{3,2,0,1:T(8,128)}, u32[]{:S(2)}, u32[]{:S(2)}) async-start(f32[2,64,64,160]{3,2,0,1:T(8,128)} %copy.104), calls=%async_computation.1 | async-start | bytes 16777216 | tf_op jit(solution)/shard_map/all_to_all | solution.py:92
  183.4 0.5 broadcast.188
  183.9 0.7 reduce.20
  185.2 44.3 %scatter_custom_fusion.1 = s32[1024]{0:T(1024)S(1)} fusion(s32[8192]{0:T(1024)S(1)} %bitcast.40, s32[8192]{0:T(1024)S(1)} %broadcast.161, s32[]{:T(128)} %constant.19.clone.1), kind=kCustom, calls=%fused_computation.74 | custom fusion | flops 8192 | bytes 4100
  229.5 139.6 %all-to-all-done.1 = f32[2,64,64,160]{3,2,0,1:T(8,128)} async-done(((f32[2,64,64,160]{3,2,0,1:T(8,128)}), f32[2,64,64,160]{3,2,0,1:T(8,128)}, u32[]{:S(2)}, u32[]{:S(2)}) %all-to-all-start.1) | async-done | bytes 5242912 | tf_op jit(solution)/shard_map/all_to_all | solution.py:92
  369.1 7.7 %copy.119 = f32[2,64,64,160]{3,2,1,0:T(8,128)} copy(f32[2,64,64,160]{3,2,0,1:T(8,128)} %all-to-all-done.1) | data formatting | bytes 10485760 | tf_op jit(solution)/shard_map/reshape | solution.py:96
  376.8 44.9 %scatter_custom_fusion.3 = f32[1024,160]{1,0:T(8,128)S(1)} fusion(s32[8192]{0:T(1024)S(1)} %bitcast.41, f32[8192,160]{1,0:T(8,128)} %bitcast.33, f32[]{:T(128)} %constant.26.clone.1), kind=kCustom, calls=%fused_computation.48 | custom fusion | flops 1310720 | bytes 655872
  421.7 0.6 copy.120
  422.3 4.0 broadcast_select_fusion
  426.4 1.0 copy.113
  427.3 1.0 copy.114
  428.3 1.0 copy.115
  (49 shorter events, 1.0 us)
Async XLA Ops:
  7.2 15.8 %copy-start = (bf16[1280,640]{1,0:T(8,128)(2,1)S(1)}, bf16[1280,640]{1,0:T(8,128)(2,1)}, u32[]{:S(2)}) copy-start(bf16[1280,640]{1,0:T(8,128)(2,1)} %param.14) | copy-start | bytes 4915204
  7.2 8.3 %copy-start.2 = (bf16[1024,640]{1,0:T(8,128)(2,1)S(1)}, bf16[1024,640]{1,0:T(8,128)(2,1)}, u32[]{:S(2)}) copy-start(bf16[1024,640]{1,0:T(8,128)(2,1)} %param.10) | copy-start | bytes 3932164
  7.2 139.7 %all-reduce.2.cloned.1.call-start = ((), (), s32[]{:S(2)}) async-start(), calls=%async_computation.2 | async-start | bytes 10485760 | tf_op jit(solution)/shard_map/psum | solution.py:70
  8.1 7.3 %collective-permute-start = (bf16[9,640]{1,0:T(8,128)(2,1)S(1)}, bf16[9,640]{1,0:T(8,128)(2,1)S(1)}, u32[]{:S(2)}, u32[]{:S(2)}) collective-permute-start(bf16[9,640]{1,0:T(8,128)(2,1)S(1)} %slice.42), channel_id=1, source_target_pairs={{0,4},{4,8},{8,12},{12,16},{16,20},{20,24},{24,28},{28,32},{32,36}... | collective-permute-start | bytes 34568 | tf_op jit(solution)/shard_map/ppermute | solution.py:16
  15.5 7.5 %copy-start.10 = (f32[1024]{0:T(1024)S(1)}, f32[1024]{0:T(1024)}, u32[]{:S(2)}) copy-start(f32[1024]{0:T(1024)} %param.12) | copy-start | bytes 12292
  17.6 5.3 %collective-permute-start.1 = (f32[9,640]{1,0:T(8,128)S(1)}, f32[9,640]{1,0:T(8,128)S(1)}, u32[]{:S(2)}, u32[]{:S(2)}) collective-permute-start(f32[9,640]{1,0:T(8,128)S(1)} %slice.56), channel_id=1, source_target_pairs={{4,0},{8,4},{12,8},{16,12},{20,16},{24,20},{28,24},{32,28},{36,32}... | collective-permute-start | bytes 69128 | tf_op jit(solution)/shard_map/ppermute | solution.py:16
  29.7 0.7 copy-start.4
  29.7 2.9 copy-start.8
  29.7 3.0 copy-start.9
  29.7 3.1 copy-start.5
  41.8 130.3 %all-to-all-start = ((s32[64,1,128]{2,1,0:T(1,128)}), s32[64,1,128]{2,1,0:T(1,128)S(1)}, u32[]{:S(2)}, u32[]{:S(2)}) async-start(s32[64,1,128]{2,1,0:T(1,128)} %reshape.147), calls=%async_computation | async-start | bytes 65536 | tf_op jit(solution)/shard_map/all_to_all | solution.py:93
  172.2 12.7 %copy-start.7 = (s32[2]{0:T(128)S(1)}, s32[2]{0:T(128)}, u32[]{:S(2)}) copy-start(s32[2]{0:T(128)} %constant.63) | copy-start | bytes 28
  172.2 12.8 %copy-start.6 = (s32[2]{0:T(128)S(1)}, s32[2]{0:T(128)}, u32[]{:S(2)}) copy-start(s32[2]{0:T(128)} %constant.66) | copy-start | bytes 28
  172.2 196.9 %all-to-all-start.1 = ((f32[2,64,64,160]{3,2,0,1:T(8,128)}), f32[2,64,64,160]{3,2,0,1:T(8,128)}, u32[]{:S(2)}, u32[]{:S(2)}) async-start(f32[2,64,64,160]{3,2,0,1:T(8,128)} %copy.104), calls=%async_computation.1 | async-start | bytes 16777216 | tf_op jit(solution)/shard_map/all_to_all | solution.py:92
  376.8 45.5 %copy-start.3 = (f32[2,512,160]{1,2,0:T(8,128)S(1)}, f32[2,512,160]{1,2,0:T(8,128)}, u32[]{:S(2)}) copy-start(f32[2,512,160]{1,2,0:T(8,128)} %param.19) | copy-start | bytes 1966084
  422.3 6.9 %copy-start.1 = (bf16[1280,640]{1,0:T(8,128)(2,1)S(1)}, bf16[1280,640]{1,0:T(8,128)(2,1)}, u32[]{:S(2)}) copy-start(bf16[1280,640]{1,0:T(8,128)(2,1)} %param.14) | copy-start | bytes 4915204
Sparse Core Ops, SparseCore 0:
  29.9 117.0 all-reduce.1
where the time goes:
time: 437 us; the launch traced here: 436 us
  waiting for transfers between devices  236 us (54%)
  other arithmetic  100 us (23%)
  local copies, waits for them, and re-layouts  48.5 us (11%)
  starting transfers between devices  29.7 us (7%)
  between operations  14.4 us (3%)
  matrix products  6.78 us (2%)
    all_to_all x1, waiting for transfers between devices, shards(): lax.all_to_all(send_grad, 'seq', split_axis=1, concat_axis=1, tiled=True)  140 us
    psum x1, waiting for transfers between devices, shards(): summed = lax.psum(full_term, 'tab')  93.5 us
    unnamed x9, other arithmetic  89.7 us
    unnamed x32, local copies, waits for them, and re-layouts  25.7 us
    all_to_all x1, starting transfers between devices, shards(): lax.all_to_all(send_rows, 'seq', split_axis=1, concat_axis=1, tiled=True)  11.6 us
    all_to_all x1, starting transfers between devices, shards(): lax.all_to_all(send_grad, 'seq', split_axis=1, concat_axis=1, tiled=True)  11.2 us
  transfers between devices with their start and end apart: 5, of which 3 were waited for; matrix products, arithmetic and copies ran while one was open for 19% of the time, Pallas kernels for 0%

commit v1 on v0

--- a/solution.py
+++ b/solution.py
@@ -8,6 +8,12 @@
 learn_rate = 0.01
 adam_steps = 10.0
 epsilon = 1e-08
+
+
+def summed_here(shard, mesh_axis):
+    shards = lax.all_gather(shard, mesh_axis, axis=0, tiled=False)
+    result = shards.sum(axis=0)
+    return result
 
 
 def from_behind(block, axis, distance):
@@ -67,7 +73,7 @@
     full_term = lax.dot_general(
         value_weight, scaled, (((1,), (1,)), ((), ())), preferred_element_type=jnp.float32
     )
-    summed = lax.psum(full_term, "tab")
+    summed = summed_here(full_term, "tab")
     memory_grad = lax.dynamic_slice_in_dim(summed, lax.axis_index("tab") * own_width, own_width, 0)
     heads_grad = jnp.swapaxes(memory_grad.reshape(head_local, head_dim, length), 1, 2)
     owners = owner_ids[:, :, 0]

time: 437 us -> 571 us (1.31)
  waiting for transfers between devices: 236 us -> 313 us
  other arithmetic: 100 us -> 132 us
  local copies, waits for them, and re-layouts: 48.5 us -> 73.8 us
    all_gather x0 -> x1, waiting for transfers between devices: none -> 171 us  [summed_here(): shards = lax.all_gather(shard, mesh_axis, axis=0, tiled=False)]
    psum x1 -> x0, waiting for transfers between devices: 93.5 us -> none  [shards(): summed = lax.psum(full_term, 'tab')]
    reduce_sum x0 -> x1, other arithmetic: none -> 31.1 us  [summed_here(): result = shards.sum(axis=0)]
    all_gather x0 -> x1, local copies, waits for them, and re-layouts: none -> 25.3 us  [summed_here(): shards = lax.all_gather(shard, mesh_axis, axis=0, tiled=False)]
  transfers between devices with their start and end apart: 5 -> 5, of which waited for: 3 -> 3; matrix products, arithmetic and copies ran while one was open for 19% -> 25% of each run, Pallas kernels for 0% -> 0%
where the time goes in v1:
time: 571 us; the launch traced here: 570 us
  waiting for transfers between devices  313 us (55%)
  other arithmetic  132 us (23%)
  local copies, waits for them, and re-layouts  73.8 us (13%)
  starting transfers between devices  29.7 us (5%)
  between operations  14.4 us (3%)
  matrix products  6.76 us (1%)
    all_gather x1, waiting for transfers between devices, summed_here(): shards = lax.all_gather(shard, mesh_axis, axis=0, tiled=False)  171 us
    all_to_all x1, waiting for transfers between devices, shards(): lax.all_to_all(send_grad, 'seq', split_axis=1, concat_axis=1, tiled=True)  139 us
    unnamed x9, other arithmetic  89.9 us
    reduce_sum x1, other arithmetic, summed_here(): result = shards.sum(axis=0)  31.1 us
    unnamed x32, local copies, waits for them, and re-layouts  25.7 us
    all_gather x1, local copies, waits for them, and re-layouts, summed_here(): shards = lax.all_gather(shard, mesh_axis, axis=0, tiled=False)  25.3 us
    all_to_all x1, starting transfers between devices, shards(): lax.all_to_all(send_rows, 'seq', split_axis=1, concat_axis=1, tiled=True)  11.6 us
  transfers between devices with their start and end apart: 5, of which 3 were waited for; matrix products, arithmetic and copies ran while one was open for 25% of the time, Pallas kernels for 0%

profile of v1, /device:TPU:1, one launch (start us, length us, event | category | flops | bytes accessed | tf_op | source)
XLA Modules:
  0.0 569.5 jit_solution(7509010087166068284)
XLA Ops:
  7.2 0.9 slice.42
  8.1 4.9 collective-permute-start
  13.0 0.9 slice_reduce_fusion.3
  13.9 1.5 convert_element_type.17
  15.5 2.1 fusion.2
  17.6 1.9 collective-permute-start.1
  19.5 3.4 collective-permute-done.1
  22.9 6.8 %convolution_bitcast_fusion = f32[1280,1024]{0,1:T(8,128)} fusion(bf16[1280,640]{1,0:T(8,128)(2,1)S(1)} %copy-done, bf16[1024,640]{1,0:T(8,128)(2,1)S(1)} %copy-done.2, f32[9,640]{1,0:T(8,128)S(1)} %collective-permute-done.1, f32[1024,640]{1,0:T(8,128)S(1)} %fusion.2, f32[640]{0:T(1024)S(1)} %get-tuple-element.23, f32[640]{0:T(1024)S(1)} %get-tuple-element.24, ...), kind=kOutput, calls=%fused_computation.5 | convolution fusion | flops 1686896640 | bytes 10850816 | tf_op jit(solution)/shard_map/dot_general | solution.py:73
  29.7 0.7 copy-done.4
  30.7 1.9 convert_reduce_fusion
  32.9 8.1 %scatter_custom_fusion = s32[8192]{0:T(1024)S(1)} fusion(s32[2048]{0:T(1024)S(1)} %get-tuple-element.29, s32[2048]{0:T(1024)S(1)} %get-tuple-element.28, s32[]{:T(128)} %constant.19.clone.1), kind=kCustom, calls=%fused_computation.60 | custom fusion | bytes 32772
  41.1 0.7 reshape.148
  41.8 11.6 %all-to-all-start = ((s32[64,1,128]{2,1,0:T(1,128)}), s32[64,1,128]{2,1,0:T(1,128)S(1)}, u32[]{:S(2)}, u32[]{:S(2)}) async-start(s32[64,1,128]{2,1,0:T(1,128)} %reshape.148), calls=%async_computation | async-start | bytes 65536 | tf_op jit(solution)/shard_map/all_to_all | solution.py:99
  53.5 170.6 %all-gather.3.cloned.1.call-done = f32[5120,1024]{0,1:T(8,128)} async-done(((f32[1280,1024]{0,1:T(8,128)}), f32[5120,1024]{0,1:T(8,128)}) %all-gather.3.cloned.1.call-update) | async-done | bytes 20971536 | tf_op jit(solution)/shard_map/all_gather | solution.py:14
  224.1 25.3 %reshape.134 = f32[4,1280,1024]{1,0,2:T(4,128)} reshape(f32[5120,1024]{0,1:T(8,128)} %all-gather.3.cloned.1.call-done) | data formatting | bytes 41943040 | tf_op jit(solution)/shard_map/all_gather | solution.py:14
  249.3 31.1 %reduce_sum.22 = f32[1280,1024]{0,1:T(8,128)} reduce(f32[4,1280,1024]{1,0,2:T(4,128)} %reshape.134, f32[]{:T(128)} %constant.26.clone.1), dimensions={0}, to_apply=%region_3.0 | reduce | flops 3932160 | bytes 26214404 | tf_op jit(solution)/shard_map/reduce_sum | solution.py:15
  280.4 2.1 constant_dynamic-slice_fusion
  282.9 1.8 copy.113
  284.8 13.2 %scatter_custom_fusion.2 = f32[8192,160]{1,0:T(8,128)} fusion(s32[2048]{0:T(1024)S(1)} %get-tuple-element.29, f32[2048,160]{1,0:T(8,128)} %bitcast.38, f32[]{:T(128)} %constant.26.clone.1), kind=kCustom, calls=%fused_computation.6 | custom fusion | bytes 5243392
  297.9 7.7 %copy.101 = f32[2,64,64,160]{3,2,0,1:T(8,128)} copy(f32[2,64,64,160]{3,2,1,0:T(8,128)} %bitcast.34) | data formatting | bytes 10485760 | tf_op jit(solution)/shard_map/reshape | solution.py:96
  305.6 11.2 %all-to-all-start.1 = ((f32[2,64,64,160]{3,2,0,1:T(8,128)}), f32[2,64,64,160]{3,2,0,1:T(8,128)}, u32[]{:S(2)}, u32[]{:S(2)}) async-start(f32[2,64,64,160]{3,2,0,1:T(8,128)} %copy.101), calls=%async_computation.1 | async-start | bytes 16777216 | tf_op jit(solution)/shard_map/all_to_all | solution.py:98
  316.8 0.5 broadcast.188
  317.4 0.7 reduce.20
  318.7 44.5 %scatter_custom_fusion.1 = s32[1024]{0:T(1024)S(1)} fusion(s32[8192]{0:T(1024)S(1)} %bitcast.42, s32[8192]{0:T(1024)S(1)} %broadcast.161, s32[]{:T(128)} %constant.19.clone.1), kind=kCustom, calls=%fused_computation.74 | custom fusion | flops 8192 | bytes 4100
  363.2 139.3 %all-to-all-done.1 = f32[2,64,64,160]{3,2,0,1:T(8,128)} async-done(((f32[2,64,64,160]{3,2,0,1:T(8,128)}), f32[2,64,64,160]{3,2,0,1:T(8,128)}, u32[]{:S(2)}, u32[]{:S(2)}) %all-to-all-start.1) | async-done | bytes 5242912 | tf_op jit(solution)/shard_map/all_to_all | solution.py:98
  502.6 7.7 %copy.116 = f32[2,64,64,160]{3,2,1,0:T(8,128)} copy(f32[2,64,64,160]{3,2,0,1:T(8,128)} %all-to-all-done.1) | data formatting | bytes 10485760 | tf_op jit(solution)/shard_map/reshape | solution.py:102
  510.3 44.9 %scatter_custom_fusion.3 = f32[1024,160]{1,0:T(8,128)S(1)} fusion(s32[8192]{0:T(1024)S(1)} %bitcast.43, f32[8192,160]{1,0:T(8,128)} %bitcast.35, f32[]{:T(128)} %constant.26.clone.1), kind=kCustom, calls=%fused_computation.48 | custom fusion | flops 1310720 | bytes 655872
  555.2 0.6 copy.117
  555.8 4.0 broadcast_select_fusion
  559.8 1.0 copy.110
  560.8 1.0 copy.111
  561.7 1.0 copy.112
  (51 shorter events, 1.8 us)
Async XLA Ops:
  7.2 15.8 %copy-start = (bf16[1280,640]{1,0:T(8,128)(2,1)S(1)}, bf16[1280,640]{1,0:T(8,128)(2,1)}, u32[]{:S(2)}) copy-start(bf16[1280,640]{1,0:T(8,128)(2,1)} %param.14) | copy-start | bytes 4915204
  7.2 8.3 %copy-start.2 = (bf16[1024,640]{1,0:T(8,128)(2,1)S(1)}, bf16[1024,640]{1,0:T(8,128)(2,1)}, u32[]{:S(2)}) copy-start(bf16[1024,640]{1,0:T(8,128)(2,1)} %param.10) | copy-start | bytes 3932164
  7.2 216.9 %all-gather.3.cloned.1.call-start = ((), (), s32[]{:S(2)}) async-start(), calls=%async_computation.2 | async-start | bytes 26214400 | tf_op jit(solution)/shard_map/all_gather | solution.py:14
  8.1 7.3 %collective-permute-start = (bf16[9,640]{1,0:T(8,128)(2,1)S(1)}, bf16[9,640]{1,0:T(8,128)(2,1)S(1)}, u32[]{:S(2)}, u32[]{:S(2)}) collective-permute-start(bf16[9,640]{1,0:T(8,128)(2,1)S(1)} %slice.42), channel_id=1, source_target_pairs={{0,4},{4,8},{8,12},{12,16},{16,20},{20,24},{24,28},{28,32},{32,36}... | collective-permute-start | bytes 34568 | tf_op jit(solution)/shard_map/ppermute | solution.py:22
  15.5 7.5 %copy-start.10 = (f32[1024]{0:T(1024)S(1)}, f32[1024]{0:T(1024)}, u32[]{:S(2)}) copy-start(f32[1024]{0:T(1024)} %param.12) | copy-start | bytes 12292
  17.6 5.3 collective-permute-start.1
  29.7 0.7 copy-start.4
  29.7 2.9 copy-start.8
  29.7 3.0 copy-start.9
  29.7 3.1 copy-start.5
  41.8 263.8 %all-to-all-start = ((s32[64,1,128]{2,1,0:T(1,128)}), s32[64,1,128]{2,1,0:T(1,128)S(1)}, u32[]{:S(2)}, u32[]{:S(2)}) async-start(s32[64,1,128]{2,1,0:T(1,128)} %reshape.148), calls=%async_computation | async-start | bytes 65536 | tf_op jit(solution)/shard_map/all_to_all | solution.py:99
  305.6 12.7 %copy-start.7 = (s32[2]{0:T(128)S(1)}, s32[2]{0:T(128)}, u32[]{:S(2)}) copy-start(s32[2]{0:T(128)} %constant.64) | copy-start | bytes 28
  305.6 12.8 %copy-start.6 = (s32[2]{0:T(128)S(1)}, s32[2]{0:T(128)}, u32[]{:S(2)}) copy-start(s32[2]{0:T(128)} %constant.67) | copy-start | bytes 28
  305.6 196.9 %all-to-all-start.1 = ((f32[2,64,64,160]{3,2,0,1:T(8,128)}), f32[2,64,64,160]{3,2,0,1:T(8,128)}, u32[]{:S(2)}, u32[]{:S(2)}) async-start(f32[2,64,64,160]{3,2,0,1:T(8,128)} %copy.101), calls=%async_computation.1 | async-start | bytes 16777216 | tf_op jit(solution)/shard_map/all_to_all | solution.py:98
  510.3 45.5 %copy-start.3 = (f32[2,512,160]{1,2,0:T(8,128)S(1)}, f32[2,512,160]{1,2,0:T(8,128)}, u32[]{:S(2)}) copy-start(f32[2,512,160]{1,2,0:T(8,128)} %param.19) | copy-start | bytes 1966084
  555.8 6.9 %copy-start.1 = (bf16[1280,640]{1,0:T(8,128)(2,1)S(1)}, bf16[1280,640]{1,0:T(8,128)(2,1)}, u32[]{:S(2)}) copy-start(bf16[1280,640]{1,0:T(8,128)(2,1)} %param.14) | copy-start | bytes 4915204
Sparse Core Ops, SparseCore 0:
  29.8 194.1 all-gather.2
